TPU v7x, 128 devices: a whole 4x4x4 slice. The times are simulated.
128 devices in a mesh: lat: 16 (over x, y), var: 8 (over z, core).
Axes of the slice: x: 4, y: 4, z: 4, core: 2. Of those that a mesh axis runs over, the one named last changes fastest.
Arguments:
- patches: bfloat16 [96, 192, 1024], P('lat', 'var'), may hold values from -6 to 6
- norm_gain: float32 [1024], replicated, may hold values from 0.25 to 1.75
- input_proj: bfloat16 [1024, 3072], replicated, may hold values from -7 to 7
- output_proj: bfloat16 [1024, 1024], replicated, may hold values from -0.1875 to 0.1875
- level_scale: float32 [40, 1024], P('var'), may hold values from 0.1 to 1.9
- level_shift: float32 [40, 1024], P('var'), may hold values from -3 to 3
- head_weight: bfloat16 [40, 1024, 320], P('var', 'lat'), may hold values from -0.1875 to 0.1875
- targets: bfloat16 [40, 96, 192, 320], P('var', 'lat'), may hold values from -6 to 6
- level_counts: int32 [4], replicated, may hold values from 13 to 37
- tile_dataset: int32 [16, 8], P('lat'), may hold values from 0 to 3
- slot_level: int32 [40], P('var'), may hold values from 0 to 39, as said below
Outputs:
- latent: bfloat16 [96, 192, 1024], P('lat', 'var')
- grad_latent: bfloat16 [96, 192, 1024], P('lat', 'var')
- grad_head: float32 [40, 1024, 320], P('var', 'lat')
Inputs may be any that keep to these rules, and one draw needn't show every extreme that they name: `slot_level`: for each j, slots j * 5 to (j + 1) * 5 - 1 hold the levels j * 5 to (j + 1) * 5 - 1 in some order.
All inputs are finite; a program needn't handle non-finite values.
Results may differ from a plain program's by a relative error of at most 0.012.
Values may be sent and summed in bfloat16 or wider, within the bound.
A program may use at most 128 MiB of HBM per device.

v0:
```python
import math
import jax
import jax.numpy as jnp
from jax import lax
from jax.sharding import PartitionSpec as P

HEADS = 16
WH = 6
WW = 12
EPS = 1e-05


def padded(array, sides, width, wrap):
    for axis, dim in sides:
        size, length = (lax.axis_size(axis), array.shape[dim])
        up = [(i, (i + 1) % size) for i in range(size if wrap else size - 1)]
        down = [(j, i) for i, j in up]
        last = lax.slice_in_dim(array, length - width, length, axis=dim)
        initial = lax.slice_in_dim(array, 0, width, axis=dim)
        before = lax.ppermute(last, axis, up)
        after = lax.ppermute(initial, axis, down)
        array = jnp.concatenate([before, array, after], axis=dim)
    return array


def layer_norm(values, gain):
    wide = values.astype(jnp.float32)
    average = jnp.mean(wide, axis=-1, keepdims=True)
    centred = wide - average
    variance = jnp.mean(centred * centred, axis=-1, keepdims=True)
    return (centred * lax.rsqrt(variance + EPS) * gain).astype(jnp.bfloat16)


def window_attention(query_ext, keyval, row_valid, heads):
    ext_rows, ext_cols, width = query_ext.shape
    head_size = width // heads
    win_rows = ext_rows // WH
    win_cols = ext_cols // WW

    def split(values, parts):
        shaped = values.reshape(win_rows, WH, win_cols, WW, parts, heads, head_size)
        return shaped.transpose(0, 2, 1, 3, 4, 5, 6).reshape(
            win_rows * win_cols, WH * WW, parts, heads, head_size
        )

    query_win = split(query_ext, 1)[:, :, 0]
    pairs = split(keyval, 2)
    key_win = pairs[:, :, 0]
    value_win = pairs[:, :, 1]
    key_mask = jnp.broadcast_to(
        row_valid.reshape(win_rows, 1, WH, 1), (win_rows, win_cols, WH, WW)
    ).reshape(win_rows * win_cols, WH * WW)
    scores = jnp.einsum(
        "wqhd,wkhd->whqk", query_win, key_win, preferred_element_type=jnp.float32
    ) / math.sqrt(head_size)
    scores = jnp.where(key_mask[:, None, None, :], scores, -jnp.inf)
    peak = jnp.max(scores, axis=-1, keepdims=True)
    weights = jnp.exp(scores - peak)
    probs = (weights / jnp.sum(weights, axis=-1, keepdims=True)).astype(jnp.bfloat16)
    mixed = jnp.einsum("whqk,wkhd->wqhd", probs, value_win, preferred_element_type=jnp.float32)
    return (
        mixed.reshape(win_rows, win_cols, WH, WW, width)
        .transpose(0, 2, 1, 3, 4)
        .reshape(ext_rows, ext_cols, width)
    )


def slot_terms(piece, target_rows, live_cols, level_scale, level_shift, heads_full):
    piece_wide = piece.astype(jnp.float32)
    rows = (
        piece_wide[None] * level_scale[:, None, None, :] + level_shift[:, None, None, :]
    ).astype(jnp.bfloat16)
    predicted = jnp.einsum("krnd,kdo->krno", rows, heads_full, preferred_element_type=jnp.float32)
    errors = ((predicted - target_rows.astype(jnp.float32)) * live_cols[:, None, :, None]).astype(
        jnp.bfloat16
    )
    back_grad = jnp.einsum("krno,kdo->krnd", errors, heads_full, preferred_element_type=jnp.float32)
    piece_grad = jnp.sum(back_grad * level_scale[:, None, None, :], axis=0)
    head_add = jnp.einsum("krnd,krno->dko", rows, errors, preferred_element_type=jnp.float32)
    return (piece_grad, head_add)


def local(
    patches,
    norm_gain,
    input_proj,
    output_proj,
    level_scale,
    level_shift,
    head_weight,
    targets,
    level_counts,
    tile_dataset,
    slot_level,
):
    band_rows, band_cols, width = patches.shape
    half_rows = WH // 2
    half_cols = WW // 2
    lat_count = lax.axis_size("lat")
    var_count = lax.axis_size("var")
    lat_place = lax.axis_index("lat")
    ext_rows = band_rows + WH
    ext_cols = band_cols + WW
    extended = padded(patches, (("lat", 0),), half_rows, False)
    extended = padded(extended, (("var", 1),), half_cols, True)
    normed_ext = layer_norm(extended, norm_gain)
    keyval = jnp.dot(
        normed_ext.reshape(-1, width), input_proj[:, width:], preferred_element_type=jnp.float32
    )
    keyval = keyval.astype(jnp.bfloat16).reshape(ext_rows, ext_cols, 2 * width)
    normed = normed_ext[half_rows : half_rows + band_rows, half_cols : half_cols + band_cols]
    queries = jnp.dot(
        normed.reshape(-1, width), input_proj[:, :width], preferred_element_type=jnp.float32
    )
    queries = queries.astype(jnp.bfloat16).reshape(band_rows, band_cols, width)
    query_ext = jnp.pad(queries, ((half_rows, WH - half_rows), (half_cols, WW - half_cols), (0, 0)))
    global_row = lat_place * band_rows - half_rows + jnp.arange(ext_rows, dtype=jnp.int32)
    row_valid = (global_row >= 0) & (global_row < lat_count * band_rows)
    mixed = window_attention(query_ext, keyval, row_valid, HEADS)
    attn = mixed[half_rows : half_rows + band_rows, half_cols : half_cols + band_cols].astype(
        jnp.bfloat16
    )
    update = jnp.dot(
        attn.reshape(-1, width), output_proj, preferred_element_type=jnp.float32
    ).reshape(band_rows, band_cols, width)
    latent = (patches.astype(jnp.float32) + update).astype(jnp.bfloat16)
    dataset_row = tile_dataset[0]
    dataset_ids = jnp.arange(level_counts.shape[0], dtype=jnp.int32)
    tile_levels = jnp.sum(
        jnp.where(dataset_row[:, None] == dataset_ids[None, :], level_counts[None, :], 0), axis=1
    )
    live_tiles = (slot_level[None, :] < tile_levels[:, None]).astype(jnp.float32)
    heads_full = lax.all_gather(head_weight, "lat", axis=1, tiled=True)
    tile_ids = jnp.arange(var_count, dtype=jnp.int32)
    piece = lax.all_gather(latent, "var", axis=1, tiled=True)
    piece_cols = piece.shape[1]
    column_tile = jnp.arange(piece_cols, dtype=jnp.int32) // band_cols
    onehot = (column_tile[:, None] == tile_ids[None, :]).astype(jnp.float32)
    column_live = jnp.dot(onehot, live_tiles)
    piece_grad, head_add = slot_terms(
        piece, targets, column_live.T, level_scale, level_shift, heads_full
    )
    latent_terms = piece_grad
    latent_terms, head_terms = (latent_terms, head_add)
    grad_latent = lax.psum_scatter(
        latent_terms.astype(jnp.bfloat16), "var", scatter_dimension=1, tiled=True
    )
    head_terms = head_terms * (1.0 / math.sqrt(lat_count * band_rows * var_count * band_cols))
    share_rows = width // lat_count
    mine = lax.psum_scatter(
        head_terms.astype(jnp.bfloat16), "lat", scatter_dimension=0, tiled=True
    ).astype(jnp.float32)
    grad_head = jnp.transpose(mine, (1, 0, 2))
    return (latent, grad_latent, grad_head)


def solution(mesh):
    in_specs = (
        P("lat", "var", None),
        P(),
        P(),
        P(),
        P("var", None),
        P("var", None),
        P("var", "lat", None),
        P("var", "lat", None, None),
        P(),
        P("lat", None),
        P("var"),
    )
    out_specs = (P("lat", "var", None), P("lat", "var", None), P("var", "lat", None))
    return jax.shard_map(local, mesh=mesh, in_specs=in_specs, out_specs=out_specs, check_vma=False)
```

profile of v0, /device:TPU:0, one launch (start us, length us, event | category | flops | bytes accessed | tf_op | source)
XLA Modules:
  0.0 313.8 jit_solution(12802649083848093492)
XLA Ops:
  8.4 3.6 %collective-permute-start = (bf16[3,24,1024]{2,1,0:T(8,128)(2,1)S(1)}, bf16[3,24,1024]{2,1,0:T(8,128)(2,1)S(1)}, u32[]{:S(2)}, u32[]{:S(2)}) collective-permute-start(bf16[3,24,1024]{2,1,0:T(8,128)(2,1)S(1)} %get-tuple-element.25), channel_id=1, source_target_pairs={{0,8},{8,16},{16,24},{24,32},{32,40},{40,48},{48,56},{56,64},{64,7... | collective-permute-start | bytes 442376 | tf_op jit(solution)/shard_map/ppermute | solution.py:20
  16.0 3.1 collective-permute-done.1
  19.3 2.9 collective-permute-start.3
  22.4 3.2 %collective-permute-done.2 = bf16[12,6,1024]{2,1,0:T(8,128)(2,1)S(1)} collective-permute-done((bf16[12,6,1024]{2,1,0:T(8,128)(2,1)S(1)}, bf16[12,6,1024]{2,1,0:T(8,128)(2,1)S(1)}, u32[]{:S(2)}, u32[]{:S(2)}) %collective-permute-start.2) | collective-permute-done | bytes 147488 | tf_op jit(solution)/shard_map/ppermute | solution.py:20
  29.7 2.7 reshape.102
  38.0 3.2 %copy.48 = bf16[2,3,6,12,1,16,64]{6,5,3,2,1,0,4:T(8,128)(2,1)} copy(bf16[2,3,6,12,1,16,64]{6,5,3,1,2,0,4:T(8,128)(2,1)} %bitcast.58) | data formatting | bytes 1769472 | tf_op jit(solution)/shard_map/transpose | solution.py:42
  41.2 5.5 %fusion.15 = bf16[432,2048]{1,0:T(8,128)(2,1)} fusion(bf16[1024,3072]{1,0:T(8,128)(2,1)} %param.13, f32[432,1024]{1,0:T(8,128)S(1)} %copy-done.2, f32[1024]{0:T(1024)S(1)} %copy-done.4, f32[432]{0:T(512)S(1)} %rsqrt.13, f32[432]{0:T(512)S(1)} %div.33), kind=kOutput, calls=%fused_computation.22 | convolution fusion | flops 1814593536 | bytes 7740800 | tf_op jit(solution)/shard_map/dot_general | solution.py:107
  46.8 6.4 %reshape_reshape.3 = bf16[2,6,3,12,2,16,64]{6,5,4,3,2,1,0:T(8,128)(2,1)} reshape(bf16[432,2048]{1,0:T(8,128)(2,1)} %fusion.15) | data formatting | bytes 3538944 | tf_op jit(solution)/shard_map/reshape;reshape | solution.py:41
  53.1 2.6 copy.46
  55.7 2.6 fusion.59
  58.3 4.0 %copy.61 = bf16[6,72,1,16,64]{1,4,3,0,2:T(8,128)(2,1)} copy(bf16[6,72,1,16,64]{4,3,2,1,0:T(8,128)(2,1)} %get-tuple-element.18) | data formatting | bytes 1769472
  62.4 4.0 %copy.62 = bf16[6,72,1,16,64]{1,4,3,0,2:T(8,128)(2,1)} copy(bf16[6,72,1,16,64]{4,3,2,1,0:T(8,128)(2,1)} %get-tuple-element.19) | data formatting | bytes 1769472
  66.4 3.1 fusion.25
  73.2 4.0 %copy.52 = bf16[6,72,16,64]{3,2,1,0:T(8,128)(2,1)} copy(bf16[6,72,16,64]{1,3,2,0:T(8,128)(2,1)} %fusion.34) | data formatting | bytes 1769472 | tf_op jit(solution)/shard_map/whqk,wkhd->wqhd/transpose | solution.py:60
  77.2 3.9 %reshape.100 = bf16[2,3,6,12,1024]{4,3,2,1,0:T(8,128)(2,1)} reshape(bf16[6,72,16,64]{3,2,1,0:T(8,128)(2,1)} %copy.52) | data formatting | bytes 1769472 | tf_op jit(solution)/shard_map/reshape | solution.py:62
  87.1 28.5 %all-gather.3.cloned.1.call-done = bf16[6,192,1024]{2,1,0:T(8,128)(2,1)} async-done(((bf16[6,24,1024]{2,1,0:T(8,128)(2,1)}), bf16[6,192,1024]{2,1,0:T(8,128)(2,1)}) %all-gather.3.cloned.1.call-update) | async-done | bytes 2359312 | tf_op jit(solution)/shard_map/all_gather | solution.py:135
  115.6 4.3 %convert_element_type.67 = f32[6,192,1024]{2,1,0:T(8,128)} convert(bf16[6,192,1024]{2,1,0:T(8,128)(2,1)} %all-gather.3.cloned.1.call-done) | non-fusion elementwise | flops 1179648 | bytes 7077888 | tf_op jit(solution)/shard_map/convert_element_type | solution.py:69
  119.9 48.6 %all-gather.5.cloned.1.call-done = bf16[5,1024,320]{2,1,0:T(8,128)(2,1)} async-done(((bf16[5,64,320]{2,1,0:T(8,128)(2,1)}), bf16[5,1024,320]{2,1,0:T(8,128)(2,1)}) %all-gather.5.cloned.1.call-update) | async-done | bytes 3276816 | tf_op jit(solution)/shard_map/all_gather | solution.py:133
  168.5 10.6 %multiply_convert_fusion = bf16[5,6,192,320]{3,2,1,0:T(8,128)(2,1)S(1)} fusion(bf16[5,6,192,320]{3,2,1,0:T(8,128)(2,1)} %param.18, f32[5,192]{1,0:T(8,128)S(1)} %fusion.52, bf16[5,1024,320]{2,1,0:T(8,128)(2,1)} %all-gather.5.cloned.1.call-done, f32[5,1024]{1,0:T(8,128)S(1)} %copy-done.7, f32[5,1024]{1,0:T(8,128)S(1)} %copy-done.6, ...), kind=kOutput, calls=%fused_computation.11 | convolution fusion | flops 3799941120 | bytes 15412992 | tf_op jit(solution)/shard_map/krnd,kdo->krno/dot_general | solution.py:73
  179.2 7.2 %multiply_reduce_fusion = bf16[6,192,1024]{2,1,0:T(8,128)(2,1)S(1)} fusion(f32[5,1024]{1,0:T(8,128)S(1)} %copy-done.6, bf16[5,6,192,320]{3,2,1,0:T(8,128)(2,1)S(1)} %multiply_convert_fusion, bf16[5,1024,320]{2,1,0:T(8,128)(2,1)S(1)} %copy-done.5), kind=kOutput, calls=%fused_computation.1 | convolution fusion | flops 3785490432 | bytes 9342976 | tf_op jit(solution)/shard_map/krno,kdo->krnd/dot_general | solution.py:77
  188.2 9.3 %fusion.14 = bf16[1024,5,320]{0,2,1:T(8,128)(2,1)} fusion(bf16[5,6,192,320]{3,2,1,0:T(8,128)(2,1)} %copy-done.11, f32[5,1024]{1,0:T(8,128)S(1)} %copy-done.7, f32[5,1024]{1,0:T(8,128)S(1)} %copy-done.6, f32[6,192,1024]{2,1,0:T(8,128)} %convert_element_type.67), kind=kOutput, calls=%fused_computation.21 | convolution fusion | flops 3795845120 | bytes 11722752 | tf_op jit(solution)/shard_map/krnd,krno->dko/dot_general | solution.py:79
  197.5 8.2 %copy.54 = bf16[1024,5,320]{2,1,0:T(8,128)(2,1)} copy(bf16[1024,5,320]{0,2,1:T(8,128)(2,1)} %fusion.14) | data formatting | bytes 6553600 | tf_op jit(solution)/shard_map/convert_element_type | solution.py:151
  205.7 16.5 %reduce-scatter.7.cloned.1.call-done = bf16[24,6144]{1,0:T(8,128)(2,1)} async-done(((bf16[192,6144]{1,0:T(8,128)(2,1)}), bf16[24,6144]{1,0:T(8,128)(2,1)}) %reduce-scatter.7.cloned.1.call-update) | async-done | bytes 294928
  224.4 80.9 %reduce-scatter.5.cloned.1.call-done = bf16[64,5,320]{2,1,0:T(8,128)(2,1)} async-done(((bf16[1024,5,320]{2,1,0:T(8,128)(2,1)}), bf16[64,5,320]{2,1,0:T(8,128)(2,1)}) %reduce-scatter.5.cloned.1.call-update) | async-done | bytes 204816 | tf_op jit(solution)/shard_map/reduce_scatter | solution.py:150
  (69 shorter events, 30.7 us)
Async XLA Ops:
  7.2 76.4 %copy-start = (bf16[1024,1024]{1,0:T(8,128)(2,1)S(1)}, bf16[1024,1024]{1,0:T(8,128)(2,1)}, u32[]{:S(2)}) copy-start(bf16[1024,1024]{1,0:T(8,128)(2,1)} %param.14) | copy-start | bytes 6291460
  7.2 108.4 %all-gather.3.cloned.1.call-start = ((), (), s32[]{:S(2)}) async-start(), calls=%async_computation.2 | async-start | bytes 2654208 | tf_op jit(solution)/shard_map/all_gather | solution.py:135
  8.4 6.7 %collective-permute-start = (bf16[3,24,1024]{2,1,0:T(8,128)(2,1)S(1)}, bf16[3,24,1024]{2,1,0:T(8,128)(2,1)S(1)}, u32[]{:S(2)}, u32[]{:S(2)}) collective-permute-start(bf16[3,24,1024]{2,1,0:T(8,128)(2,1)S(1)} %get-tuple-element.25), channel_id=1, source_target_pairs={{0,8},{8,16},{16,24},{24,32},{32,40},{40,48},{48,56},{56,64},{64,7... | collective-permute-start | bytes 442376 | tf_op jit(solution)/shard_map/ppermute | solution.py:20
  12.0 7.2 %collective-permute-start.1 = (bf16[3,24,1024]{2,1,0:T(8,128)(2,1)S(1)}, bf16[3,24,1024]{2,1,0:T(8,128)(2,1)S(1)}, u32[]{:S(2)}, u32[]{:S(2)}) collective-permute-start(bf16[3,24,1024]{2,1,0:T(8,128)(2,1)S(1)} %get-tuple-element.24), channel_id=1, source_target_pairs={{8,0},{16,8},{24,16},{32,24},{40,32},{48,40},{56,48},{64,56},{72,6... | collective-permute-start | bytes 442376 | tf_op jit(solution)/shard_map/ppermute | solution.py:21
  19.2 6.3 %collective-permute-start.2 = (bf16[12,6,1024]{2,1,0:T(8,128)(2,1)S(1)}, bf16[12,6,1024]{2,1,0:T(8,128)(2,1)S(1)}, u32[]{:S(2)}, u32[]{:S(2)}) collective-permute-start(bf16[12,6,1024]{2,1,0:T(8,128)(2,1)S(1)} %get-tuple-element.22), channel_id=1, source_target_pairs={{0,1},{1,2},{2,3},{3,4},{4,5},{5,6},{6,7},{7,0},{8,9},{9,10},{10,1... | collective-permute-start | bytes 442376 | tf_op jit(solution)/shard_map/ppermute | solution.py:20
  19.3 6.3 %collective-permute-start.3 = (bf16[12,6,1024]{2,1,0:T(8,128)(2,1)S(1)}, bf16[12,6,1024]{2,1,0:T(8,128)(2,1)S(1)}, u32[]{:S(2)}, u32[]{:S(2)}) collective-permute-start(bf16[12,6,1024]{2,1,0:T(8,128)(2,1)S(1)} %get-tuple-element.23), channel_id=1, source_target_pairs={{1,0},{2,1},{3,2},{4,3},{5,4},{6,5},{7,6},{0,7},{9,8},{10,9},{11,1... | collective-permute-start | bytes 442376 | tf_op jit(solution)/shard_map/ppermute | solution.py:21
  27.9 4.5 %copy-start.4 = (f32[1024]{0:T(1024)S(1)}, f32[1024]{0:T(1024)}, u32[]{:S(2)}) copy-start(f32[1024]{0:T(1024)} %param.12) | copy-start | bytes 12292
  38.0 3.2 %copy-start.2 = (f32[432,1024]{1,0:T(8,128)S(1)}, f32[432,1024]{1,0:T(8,128)}, u32[]{:S(2)}) copy-start(f32[432,1024]{1,0:T(8,128)} %reshape.102) | copy-start | bytes 5308420
  69.5 1.8 copy-start.3
  82.5 4.2 %copy-start.8 = (s32[4]{0:T(128)S(1)}, s32[4]{0:T(128)}, u32[]{:S(2)}) copy-start(s32[4]{0:T(128)} %param.19) | copy-start | bytes 52
  82.5 4.2 %copy-start.9 = (s32[1,8]{1,0:T(1,128)S(1)}, s32[1,8]{1,0:T(1,128)}, u32[]{:S(2)}) copy-start(s32[1,8]{1,0:T(1,128)} %param.20) | copy-start | bytes 100
  82.5 4.3 %copy-start.10 = (s32[5]{0:T(128)S(1)}, s32[5]{0:T(128)}, u32[]{:S(2)}) copy-start(s32[5]{0:T(128)} %param.21) | copy-start | bytes 64
  85.9 82.6 %all-gather.5.cloned.1.call-start = ((), (), s32[]{:S(2)}) async-start(), calls=%async_computation.3 | async-start | bytes 4177920 | tf_op jit(solution)/shard_map/all_gather | solution.py:133
  86.6 135.5 %reduce-scatter.7.cloned.1.call-start = ((), (), s32[]{:S(2)}) async-start(), calls=%async_computation.5 | async-start | bytes 2654208
  87.1 81.5 %copy-start.6 = (f32[5,1024]{1,0:T(8,128)S(1)}, f32[5,1024]{1,0:T(8,128)}, u32[]{:S(2)}) copy-start(f32[5,1024]{1,0:T(8,128)} %param.15) | copy-start | bytes 61444
  87.1 81.5 %copy-start.7 = (f32[5,1024]{1,0:T(8,128)S(1)}, f32[5,1024]{1,0:T(8,128)}, u32[]{:S(2)}) copy-start(f32[5,1024]{1,0:T(8,128)} %param.16) | copy-start | bytes 61444
  168.5 10.6 %copy-start.5 = (bf16[5,1024,320]{2,1,0:T(8,128)(2,1)S(1)}, bf16[5,1024,320]{2,1,0:T(8,128)(2,1)}, u32[]{:S(2)}) copy-start(bf16[5,1024,320]{2,1,0:T(8,128)(2,1)} %all-gather.5.cloned.1.call-done) | copy-start | bytes 9830404
  179.2 7.2 %copy-start.11 = (bf16[5,6,192,320]{3,2,1,0:T(8,128)(2,1)}, bf16[5,6,192,320]{3,2,1,0:T(8,128)(2,1)S(1)}, u32[]{:S(2)}) copy-start(bf16[5,6,192,320]{3,2,1,0:T(8,128)(2,1)S(1)} %multiply_convert_fusion) | copy-start | bytes 11059204
  188.1 117.2 %reduce-scatter.5.cloned.1.call-start = ((), (), s32[]{:S(2)}) async-start(), calls=%async_computation.4 | async-start | bytes 6684672 | tf_op jit(solution)/shard_map/reduce_scatter | solution.py:150
  205.7 101.6 %copy-start.1 = (bf16[1024,1024]{1,0:T(8,128)(2,1)S(1)}, bf16[1024,1024]{1,0:T(8,128)(2,1)}, u32[]{:S(2)}) copy-start(bf16[1024,1024]{1,0:T(8,128)(2,1)} %param.14) | copy-start | bytes 6291460
Sparse Core Ops, SparseCore 0:
  86.0 29.4 all-gather.2
  117.7 50.7 all-gather.4
  188.2 33.9 reduce-scatter.6
  225.5 79.7 reduce-scatter.4
where the time goes:
time: 315 us; the launch traced here: 314 us
  waiting for transfers between devices  183 us (58%)
  local copies, waits for them, and re-layouts  53.8 us (17%)
  matrix products  42.2 us (13%)
  between operations  14 us (4%)
  other arithmetic  12.5 us (4%)
  starting transfers between devices  7.98 us (3%)
    reduce_scatter x1, waiting for transfers between devices, local(): lax.psum_scatter(head_terms.astype(jnp.bfloat16), 'lat', scatter_dimensio...  80.9 us
    all_gather x1, waiting for transfers between devices, local(): heads_full = lax.all_gather(head_weight, 'lat', axis=1, tiled=True)  48.6 us
    all_gather x1, waiting for transfers between devices, local(): piece = lax.all_gather(latent, 'var', axis=1, tiled=True)  28.5 us
    unnamed x5, waiting for transfers between devices  17.3 us
    unnamed x32, local copies, waits for them, and re-layouts  13.9 us
    dot_general x1, matrix products, slot_terms(): jnp.einsum('krnd,kdo->krno', rows, heads_full, preferred_element_type=jnp...  10.6 us
    dot_general x1, matrix products, slot_terms(): jnp.einsum('krnd,krno->dko', rows, errors, preferred_element_type=jnp.flo...  9.29 us
    another operation x2, local copies, waits for them, and re-layouts, split(): shaped = values.reshape(win_rows, WH, win_cols, WW, parts, heads, head_size)  8.98 us
  transfers between devices with their start and end apart: 8, of which 7 were waited for; matrix products, arithmetic and copies ran while one was open for 8% of the time, Pallas kernels for 0%

commit v1 on v0

--- a/solution.py
+++ b/solution.py
@@ -132,7 +132,11 @@
     live_tiles = (slot_level[None, :] < tile_levels[:, None]).astype(jnp.float32)
     heads_full = lax.all_gather(head_weight, "lat", axis=1, tiled=True)
     tile_ids = jnp.arange(var_count, dtype=jnp.int32)
-    piece = lax.all_gather(latent, "var", axis=1, tiled=True)
+    length_2 = lax.axis_size("var")
+    repeats = [length_2 if d == 1 else 1 for d in range(latent.ndim)]
+    piece = lax.all_to_all(
+        jnp.tile(latent, repeats), "var", split_axis=1, concat_axis=1, tiled=True
+    )
     piece_cols = piece.shape[1]
     column_tile = jnp.arange(piece_cols, dtype=jnp.int32) // band_cols
     onehot = (column_tile[:, None] == tile_ids[None, :]).astype(jnp.float32)

time: 315 us -> 284 us (0.902)
  waiting for transfers between devices: 183 us -> 145 us
  starting transfers between devices: 7.98 us -> 14 us
    all_gather x1, waiting for transfers between devices: 48.6 us -> 0.01 us  [local(): heads_full = lax.all_gather(head_weight, 'lat', axis=1, tiled=True)]
    all_to_all x0 -> x1, waiting for transfers between devices: none -> 37.9 us  [local(): lax.all_to_all(jnp.tile(latent, repeats), 'var', split_axis=1, concat_axi...]
    all_gather x1 -> x0, waiting for transfers between devices: 28.5 us -> none  [local(): piece = lax.all_gather(latent, 'var', axis=1, tiled=True)]
    all_to_all x0 -> x1, starting transfers between devices: none -> 5.84 us  [local(): lax.all_to_all(jnp.tile(latent, repeats), 'var', split_axis=1, concat_axi...]
    unnamed x5 -> x4, waiting for transfers between devices: 17.3 us -> 17.3 us
    unnamed x32 -> x34, local copies, waits for them, and re-layouts: 13.9 us -> 13.9 us
  transfers between devices with their start and end apart: 8 -> 8, of which waited for: 7 -> 6; matrix products, arithmetic and copies ran while one was open for 8% -> 31% of each run, Pallas kernels for 0% -> 0%
where the time goes in v1:
time: 284 us; the launch traced here: 283 us
  waiting for transfers between devices  145 us (51%)
  local copies, waits for them, and re-layouts  56 us (20%)
  matrix products  40.9 us (14%)
  starting transfers between devices  14 us (5%)
  between operations  14 us (5%)
  other arithmetic  13.5 us (5%)
    reduce_scatter x1, waiting for transfers between devices, local(): lax.psum_scatter(head_terms.astype(jnp.bfloat16), 'lat', scatter_dimensio...  81.3 us
    all_to_all x1, waiting for transfers between devices, local(): lax.all_to_all(jnp.tile(latent, repeats), 'var', split_axis=1, concat_axi...  37.9 us
    unnamed x4, waiting for transfers between devices  17.3 us
    unnamed x34, local copies, waits for them, and re-layouts  13.9 us
    dot_general x1, matrix products, slot_terms(): jnp.einsum('krnd,kdo->krno', rows, heads_full, preferred_element_type=jnp...  9.92 us
    dot_general x1, matrix products, slot_terms(): jnp.einsum('krnd,krno->dko', rows, errors, preferred_element_type=jnp.flo...  9.29 us
    another operation x2, local copies, waits for them, and re-layouts, split(): shaped = values.reshape(win_rows, WH, win_cols, WW, parts, heads, head_size)  8.98 us
    convert_element_type x1, local copies, waits for them, and re-layouts, local(): head_terms.astype(jnp.bfloat16)  8.18 us
  transfers between devices with their start and end apart: 8, of which 6 were waited for; matrix products, arithmetic and copies ran while one was open for 31% of the time, Pallas kernels for 0%

profile of v1, /device:TPU:0, one launch (start us, length us, event | category | flops | bytes accessed | tf_op | source)
XLA Modules:
  0.0 283.0 jit_solution(8168551677998861052)
XLA Ops:
  8.4 3.6 %collective-permute-start = (bf16[3,24,1024]{2,1,0:T(8,128)(2,1)S(1)}, bf16[3,24,1024]{2,1,0:T(8,128)(2,1)S(1)}, u32[]{:S(2)}, u32[]{:S(2)}) collective-permute-start(bf16[3,24,1024]{2,1,0:T(8,128)(2,1)S(1)} %get-tuple-element.28), channel_id=1, source_target_pairs={{0,8},{8,16},{16,24},{24,32},{32,40},{40,48},{48,56},{56,64},{64,7... | collective-permute-start | bytes 442376 | tf_op jit(solution)/shard_map/ppermute | solution.py:20
  16.0 3.1 %collective-permute-done.1 = bf16[3,24,1024]{2,1,0:T(8,128)(2,1)S(1)} collective-permute-done((bf16[3,24,1024]{2,1,0:T(8,128)(2,1)S(1)}, bf16[3,24,1024]{2,1,0:T(8,128)(2,1)S(1)}, u32[]{:S(2)}, u32[]{:S(2)}) %collective-permute-start.1) | collective-permute-done | bytes 147488 | tf_op jit(solution)/shard_map/ppermute | solution.py:21
  19.3 2.9 %collective-permute-start.3 = (bf16[12,6,1024]{2,1,0:T(8,128)(2,1)S(1)}, bf16[12,6,1024]{2,1,0:T(8,128)(2,1)S(1)}, u32[]{:S(2)}, u32[]{:S(2)}) collective-permute-start(bf16[12,6,1024]{2,1,0:T(8,128)(2,1)S(1)} %get-tuple-element.26), channel_id=1, source_target_pairs={{1,0},{2,1},{3,2},{4,3},{5,4},{6,5},{7,6},{0,7},{9,8},{10,9},{11,1... | collective-permute-start | bytes 442376 | tf_op jit(solution)/shard_map/ppermute | solution.py:21
  22.4 3.1 %collective-permute-done.2 = bf16[12,6,1024]{2,1,0:T(8,128)(2,1)S(1)} collective-permute-done((bf16[12,6,1024]{2,1,0:T(8,128)(2,1)S(1)}, bf16[12,6,1024]{2,1,0:T(8,128)(2,1)S(1)}, u32[]{:S(2)}, u32[]{:S(2)}) %collective-permute-start.2) | collective-permute-done | bytes 147488 | tf_op jit(solution)/shard_map/ppermute | solution.py:20
  29.7 2.7 reshape.106
  38.1 3.2 %copy.62 = bf16[2,3,6,12,1,16,64]{6,5,3,2,1,0,4:T(8,128)(2,1)} copy(bf16[2,3,6,12,1,16,64]{6,5,3,1,2,0,4:T(8,128)(2,1)} %bitcast.60) | data formatting | bytes 1769472 | tf_op jit(solution)/shard_map/transpose | solution.py:42
  41.3 5.5 %fusion.15 = bf16[432,2048]{1,0:T(8,128)(2,1)} fusion(bf16[1024,3072]{1,0:T(8,128)(2,1)} %param.13, f32[432,1024]{1,0:T(8,128)S(1)} %copy-done.2, f32[1024]{0:T(1024)S(1)} %copy-done.5, f32[432]{0:T(512)S(1)} %rsqrt.13, f32[432]{0:T(512)S(1)} %div.33), kind=kOutput, calls=%fused_computation.22 | convolution fusion | flops 1814593536 | bytes 7740800 | tf_op jit(solution)/shard_map/dot_general | solution.py:107
  46.8 6.4 %reshape_reshape.3 = bf16[2,6,3,12,2,16,64]{6,5,4,3,2,1,0:T(8,128)(2,1)} reshape(bf16[432,2048]{1,0:T(8,128)(2,1)} %fusion.15) | data formatting | bytes 3538944 | tf_op jit(solution)/shard_map/reshape;reshape | solution.py:41
  53.2 2.6 copy.60
  55.8 2.6 fusion.59
  58.4 4.0 %copy.77 = bf16[6,72,1,16,64]{1,4,3,0,2:T(8,128)(2,1)} copy(bf16[6,72,1,16,64]{4,3,2,1,0:T(8,128)(2,1)} %get-tuple-element.21) | data formatting | bytes 1769472
  62.4 4.1 %copy.78 = bf16[6,72,1,16,64]{1,4,3,0,2:T(8,128)(2,1)} copy(bf16[6,72,1,16,64]{4,3,2,1,0:T(8,128)(2,1)} %get-tuple-element.22) | data formatting | bytes 1769472
  66.5 3.1 %fusion.25 = f32[6,16,72,72]{2,3,1,0:T(8,128)S(1)} fusion(bf16[6,72,16,64]{3,2,1,0:T(8,128)(2,1)} %bitcast.61, bf16[6,72,1,16,64]{1,4,3,0,2:T(8,128)(2,1)} %copy.78), kind=kOutput, calls=%fused_computation.30 | convolution fusion | flops 63700992 | bytes 3760128 | tf_op jit(solution)/shard_map/wqhd,wkhd->whqk/dot_general | solution.py:53
  73.3 4.0 %copy.66 = bf16[6,72,16,64]{3,2,1,0:T(8,128)(2,1)} copy(bf16[6,72,16,64]{1,3,2,0:T(8,128)(2,1)} %fusion.34) | data formatting | bytes 1769472 | tf_op jit(solution)/shard_map/whqk,wkhd->wqhd/transpose | solution.py:60
  77.3 3.9 %reshape.104 = bf16[2,3,6,12,1024]{4,3,2,1,0:T(8,128)(2,1)} reshape(bf16[6,72,16,64]{3,2,1,0:T(8,128)(2,1)} %copy.66) | data formatting | bytes 1769472 | tf_op jit(solution)/shard_map/reshape | solution.py:62
  87.5 5.8 %all-to-all-start = ((bf16[6,192,1024]{2,0,1:T(8,128)(2,1)}), bf16[6,192,1024]{2,0,1:T(8,128)(2,1)}, u32[]{:S(2)}, u32[]{:S(2)}) async-start(bf16[6,192,1024]{2,0,1:T(8,128)(2,1)} %bitcast.58), calls=%async_computation | async-start | bytes 6291456 | tf_op jit(solution)/shard_map/all_to_all | solution.py:137
  94.0 37.9 %all-to-all-done = bf16[6,192,1024]{2,0,1:T(8,128)(2,1)} async-done(((bf16[6,192,1024]{2,0,1:T(8,128)(2,1)}), bf16[6,192,1024]{2,0,1:T(8,128)(2,1)}, u32[]{:S(2)}, u32[]{:S(2)}) %all-to-all-start) | async-done | bytes 2359328 | tf_op jit(solution)/shard_map/all_to_all | solution.py:137
  131.9 5.4 %copy_convert_fusion = f32[6,192,1024]{2,1,0:T(8,128)} fusion(bf16[6,192,1024]{2,0,1:T(8,128)(2,1)} %all-to-all-done), kind=kLoop, calls=%fused_computation.24 | loop fusion | flops 1179648 | bytes 7077888 | tf_op jit(solution)/shard_map/convert_element_type | solution.py:69
  137.3 9.9 %multiply_convert_fusion = bf16[5,6,192,320]{3,2,1,0:T(8,128)(2,1)S(1)} fusion(bf16[5,6,192,320]{3,2,1,0:T(8,128)(2,1)} %param.18, f32[5,192]{1,0:T(8,128)S(1)} %fusion.52, bf16[5,1024,320]{2,1,0:T(8,128)(2,1)} %all-gather.2.cloned.1.call-done, f32[5,1024]{1,0:T(8,128)S(1)} %copy-done.8, f32[5,1024]{1,0:T(8,128)S(1)} %copy-done.7, ...), kind=kOutput, calls=%fused_computation.11 | convolution fusion | flops 3799941120 | bytes 15412992 | tf_op jit(solution)/shard_map/krnd,kdo->krno/dot_general | solution.py:73
  147.3 7.2 %multiply_reduce_fusion = bf16[6,192,1024]{2,1,0:T(8,128)(2,1)S(1)} fusion(f32[5,1024]{1,0:T(8,128)S(1)} %copy-done.7, bf16[5,6,192,320]{3,2,1,0:T(8,128)(2,1)S(1)} %multiply_convert_fusion, bf16[5,1024,320]{2,1,0:T(8,128)(2,1)S(1)} %copy-done.6), kind=kOutput, calls=%fused_computation.1 | convolution fusion | flops 3785490432 | bytes 9342976 | tf_op jit(solution)/shard_map/krno,kdo->krnd/dot_general | solution.py:77
  156.3 9.3 %fusion.14 = bf16[1024,5,320]{0,2,1:T(8,128)(2,1)} fusion(bf16[5,6,192,320]{3,2,1,0:T(8,128)(2,1)} %copy-done.12, f32[5,1024]{1,0:T(8,128)S(1)} %copy-done.8, f32[5,1024]{1,0:T(8,128)S(1)} %copy-done.7, f32[6,192,1024]{2,1,0:T(8,128)} %copy_convert_fusion), kind=kOutput, calls=%fused_computation.21 | convolution fusion | flops 3795845120 | bytes 11722752 | tf_op jit(solution)/shard_map/krnd,krno->dko/dot_general | solution.py:79
  165.6 8.2 %copy.70 = bf16[1024,5,320]{2,1,0:T(8,128)(2,1)} copy(bf16[1024,5,320]{0,2,1:T(8,128)(2,1)} %fusion.14) | data formatting | bytes 6553600 | tf_op jit(solution)/shard_map/convert_element_type | solution.py:155
  173.8 17.3 %reduce-scatter.7.cloned.1.call-done = bf16[24,6144]{1,0:T(8,128)(2,1)} async-done(((bf16[192,6144]{1,0:T(8,128)(2,1)}), bf16[24,6144]{1,0:T(8,128)(2,1)}) %reduce-scatter.7.cloned.1.call-update) | async-done | bytes 294928
  193.2 81.3 %reduce-scatter.5.cloned.1.call-done = bf16[64,5,320]{2,1,0:T(8,128)(2,1)} async-done(((bf16[1024,5,320]{2,1,0:T(8,128)(2,1)}), bf16[64,5,320]{2,1,0:T(8,128)(2,1)}) %reduce-scatter.5.cloned.1.call-update) | async-done | bytes 204816 | tf_op jit(solution)/shard_map/reduce_scatter | solution.py:154
  (72 shorter events, 31.8 us)
Async XLA Ops:
  7.2 76.5 %copy-start = (bf16[1024,1024]{1,0:T(8,128)(2,1)S(1)}, bf16[1024,1024]{1,0:T(8,128)(2,1)}, u32[]{:S(2)}) copy-start(bf16[1024,1024]{1,0:T(8,128)(2,1)} %param.14) | copy-start | bytes 6291460
  7.2 130.1 %all-gather.2.cloned.1.call-start = ((), (), s32[]{:S(2)}) async-start(), calls=%async_computation.3 | async-start | bytes 4177920 | tf_op jit(solution)/shard_map/all_gather | solution.py:133
  8.4 6.7 %collective-permute-start = (bf16[3,24,1024]{2,1,0:T(8,128)(2,1)S(1)}, bf16[3,24,1024]{2,1,0:T(8,128)(2,1)S(1)}, u32[]{:S(2)}, u32[]{:S(2)}) collective-permute-start(bf16[3,24,1024]{2,1,0:T(8,128)(2,1)S(1)} %get-tuple-element.28), channel_id=1, source_target_pairs={{0,8},{8,16},{16,24},{24,32},{32,40},{40,48},{48,56},{56,64},{64,7... | collective-permute-start | bytes 442376 | tf_op jit(solution)/shard_map/ppermute | solution.py:20
  12.0 7.2 %collective-permute-start.1 = (bf16[3,24,1024]{2,1,0:T(8,128)(2,1)S(1)}, bf16[3,24,1024]{2,1,0:T(8,128)(2,1)S(1)}, u32[]{:S(2)}, u32[]{:S(2)}) collective-permute-start(bf16[3,24,1024]{2,1,0:T(8,128)(2,1)S(1)} %get-tuple-element.27), channel_id=1, source_target_pairs={{8,0},{16,8},{24,16},{32,24},{40,32},{48,40},{56,48},{64,56},{72,6... | collective-permute-start | bytes 442376 | tf_op jit(solution)/shard_map/ppermute | solution.py:21
  19.2 6.3 %collective-permute-start.2 = (bf16[12,6,1024]{2,1,0:T(8,128)(2,1)S(1)}, bf16[12,6,1024]{2,1,0:T(8,128)(2,1)S(1)}, u32[]{:S(2)}, u32[]{:S(2)}) collective-permute-start(bf16[12,6,1024]{2,1,0:T(8,128)(2,1)S(1)} %get-tuple-element.25), channel_id=1, source_target_pairs={{0,1},{1,2},{2,3},{3,4},{4,5},{5,6},{6,7},{7,0},{8,9},{9,10},{10,1... | collective-permute-start | bytes 442376 | tf_op jit(solution)/shard_map/ppermute | solution.py:20
  19.3 6.3 %collective-permute-start.3 = (bf16[12,6,1024]{2,1,0:T(8,128)(2,1)S(1)}, bf16[12,6,1024]{2,1,0:T(8,128)(2,1)S(1)}, u32[]{:S(2)}, u32[]{:S(2)}) collective-permute-start(bf16[12,6,1024]{2,1,0:T(8,128)(2,1)S(1)} %get-tuple-element.26), channel_id=1, source_target_pairs={{1,0},{2,1},{3,2},{4,3},{5,4},{6,5},{7,6},{0,7},{9,8},{10,9},{11,1... | collective-permute-start | bytes 442376 | tf_op jit(solution)/shard_map/ppermute | solution.py:21
  27.8 4.5 %copy-start.5 = (f32[1024]{0:T(1024)S(1)}, f32[1024]{0:T(1024)}, u32[]{:S(2)}) copy-start(f32[1024]{0:T(1024)} %param.12) | copy-start | bytes 12292
  38.1 3.3 %copy-start.2 = (f32[432,1024]{1,0:T(8,128)S(1)}, f32[432,1024]{1,0:T(8,128)}, u32[]{:S(2)}) copy-start(f32[432,1024]{1,0:T(8,128)} %reshape.106) | copy-start | bytes 5308420
  69.6 1.8 copy-start.3
  85.3 2.2 copy-start.4
  87.5 6.1 %copy-start.9 = (s32[4]{0:T(128)S(1)}, s32[4]{0:T(128)}, u32[]{:S(2)}) copy-start(s32[4]{0:T(128)} %param.19) | copy-start | bytes 52
  87.5 6.1 %copy-start.10 = (s32[1,8]{1,0:T(1,128)S(1)}, s32[1,8]{1,0:T(1,128)}, u32[]{:S(2)}) copy-start(s32[1,8]{1,0:T(1,128)} %param.20) | copy-start | bytes 100
  87.5 6.2 %copy-start.11 = (s32[5]{0:T(128)S(1)}, s32[5]{0:T(128)}, u32[]{:S(2)}) copy-start(s32[5]{0:T(128)} %param.21) | copy-start | bytes 64
  87.5 44.4 %all-to-all-start = ((bf16[6,192,1024]{2,0,1:T(8,128)(2,1)}), bf16[6,192,1024]{2,0,1:T(8,128)(2,1)}, u32[]{:S(2)}, u32[]{:S(2)}) async-start(bf16[6,192,1024]{2,0,1:T(8,128)(2,1)} %bitcast.58), calls=%async_computation | async-start | bytes 6291456 | tf_op jit(solution)/shard_map/all_to_all | solution.py:137
  93.4 97.6 %reduce-scatter.7.cloned.1.call-start = ((), (), s32[]{:S(2)}) async-start(), calls=%async_computation.5 | async-start | bytes 2654208
  94.0 43.3 %copy-start.7 = (f32[5,1024]{1,0:T(8,128)S(1)}, f32[5,1024]{1,0:T(8,128)}, u32[]{:S(2)}) copy-start(f32[5,1024]{1,0:T(8,128)} %param.15) | copy-start | bytes 61444
  94.0 43.3 %copy-start.8 = (f32[5,1024]{1,0:T(8,128)S(1)}, f32[5,1024]{1,0:T(8,128)}, u32[]{:S(2)}) copy-start(f32[5,1024]{1,0:T(8,128)} %param.16) | copy-start | bytes 61444
  137.3 9.9 %copy-start.6 = (bf16[5,1024,320]{2,1,0:T(8,128)(2,1)S(1)}, bf16[5,1024,320]{2,1,0:T(8,128)(2,1)}, u32[]{:S(2)}) copy-start(bf16[5,1024,320]{2,1,0:T(8,128)(2,1)} %all-gather.2.cloned.1.call-done) | copy-start | bytes 9830404
  147.3 7.2 %copy-start.12 = (bf16[5,6,192,320]{3,2,1,0:T(8,128)(2,1)}, bf16[5,6,192,320]{3,2,1,0:T(8,128)(2,1)S(1)}, u32[]{:S(2)}) copy-start(bf16[5,6,192,320]{3,2,1,0:T(8,128)(2,1)S(1)} %multiply_convert_fusion) | copy-start | bytes 11059204
  156.2 118.3 %reduce-scatter.5.cloned.1.call-start = ((), (), s32[]{:S(2)}) async-start(), calls=%async_computation.4 | async-start | bytes 6684672 | tf_op jit(solution)/shard_map/reduce_scatter | solution.py:154
  173.7 102.7 %copy-start.1 = (bf16[1024,1024]{1,0:T(8,128)(2,1)S(1)}, bf16[1024,1024]{1,0:T(8,128)(2,1)}, u32[]{:S(2)}) copy-start(bf16[1024,1024]{1,0:T(8,128)(2,1)} %param.14) | copy-start | bytes 6291460
Sparse Core Ops, SparseCore 0:
  22.3 52.7 all-gather.1
  156.3 34.6 reduce-scatter.6
  194.5 80.0 reduce-scatter.4
